TPU v7x, 32 devices: a whole 2x2x4 slice. The times are simulated.
32 devices in a mesh: blk: 2 (over x), grid: 16 (over z, y, core).
Axes of the slice: x: 2, y: 2, z: 4, core: 2. Of those that a mesh axis runs over, the one named last changes fastest.
Arguments:
- centers: bfloat16 [4096, 512], P(('blk', 'grid')), as said below
- weights: float32 [4096, 1000], P(('blk', 'grid')), may hold values from -6 to 6
- batch_index: int32 [512], replicated, may hold values from 0 to 4095, as said below
- labels: int32 [512], replicated, may hold values from 0 to 999
- sub_index: int32 [256], P(('blk', 'grid')), may hold values from 0 to 127
- eigvecs: bfloat16 [256, 160], P(('blk', 'grid')), may hold values from -0.375 to 0.375
- scales: float32 [160], replicated, may hold values from 1 to 16
Outputs:
- predictions: bfloat16 [512, 1000], replicated
- center_grad: bfloat16 [4096, 1000], P(('blk', 'grid'))
- sub_increment: float32 [256, 1000], P(('blk', 'grid'))
Inputs may be any that keep to these rules, and one draw needn't show every extreme that they name: Each device's block of 128 centers is named by exactly 512 / 32 entries of batch_index. sub_index: entry i names center (i // 8) * 128 + sub_index[i]. centers: row scales of order one.
All inputs are finite; a program needn't handle non-finite values.
Results may differ from a plain program's by a relative error of at most 0.0011.
The roundings to bfloat16 on the way count: a program that leaves them out, or rounds other values in their place, can miss the bound.
Values may be sent and summed in bfloat16 or wider, within the bound.
A program may use at most 64 MiB of HBM per device.

v0:
```python
import jax
import jax.numpy as jnp
from jax import lax
from jax.sharding import PartitionSpec as P

SOFTEN = 1.0
SPREAD = 4.0


def kernel(left, right):
    left_sq = jnp.sum(jnp.square(left.astype(jnp.float32)), axis=1)
    right_sq = jnp.sum(jnp.square(right.astype(jnp.float32)), axis=1)
    cross = lax.dot_general(
        left, right, (((1,), (1,)), ((), ())), preferred_element_type=jnp.float32
    )
    dist = jnp.sqrt(jnp.maximum(left_sq[:, None] + right_sq[None, :] - 2.0 * cross, 0.0) + SOFTEN)
    return jnp.exp(-dist / SPREAD)


def one_hot(label_rows, classes):
    return (label_rows[:, None] == jnp.arange(classes, dtype=jnp.int32)[None, :]).astype(
        jnp.float32
    )


def local(centers, weights, batch_index, labels, sub_index, eigvecs, scales):
    myself = lax.axis_index(("blk", "grid"))
    held = centers.shape[0]
    classes = weights.shape[1]
    owner = batch_index // held
    within = batch_index % held
    picked = jnp.take(centers, within, axis=0).astype(jnp.float32)
    picked = jnp.where((owner == myself)[:, None], picked, 0.0)
    batch = lax.psum(picked, ("blk", "grid")).astype(jnp.bfloat16)
    kbz = kernel(batch, centers).astype(jnp.bfloat16)
    partial_out = jnp.dot(kbz, weights.astype(jnp.bfloat16), preferred_element_type=jnp.float32)
    total = lax.psum(partial_out, ("blk", "grid"))
    predictions = total.astype(jnp.bfloat16)
    resid = (total - one_hot(labels, classes)).astype(jnp.bfloat16)
    subset_here = jnp.take(centers, sub_index, axis=0)
    sub_rows = lax.all_gather(subset_here, ("blk", "grid"), axis=0, tiled=True)
    vec_rows = lax.all_gather(eigvecs, ("blk", "grid"), axis=0, tiled=True)
    kzs = kernel(centers, sub_rows).astype(jnp.bfloat16)
    ksb_piece = kernel(sub_rows, batch).astype(jnp.bfloat16)
    kze_next = jnp.dot(kzs, vec_rows, preferred_element_type=jnp.float32)
    proj_next = lax.dot_general(
        vec_rows, ksb_piece, (((0,), (0,)), ((), ())), preferred_element_type=jnp.float32
    )
    coeff = jnp.dot(proj_next, resid.astype(jnp.float32), precision=lax.Precision.HIGHEST)
    scaled = scales[:, None] * coeff
    sub_increment = jnp.dot(eigvecs.astype(jnp.float32), scaled, precision=lax.Precision.HIGHEST)
    correction = jnp.dot(kze_next, scaled, precision=lax.Precision.HIGHEST)
    first = lax.dot_general(
        kbz, resid, (((0,), (0,)), ((), ())), preferred_element_type=jnp.float32
    )
    center_grad = (first - correction).astype(jnp.bfloat16)
    return (predictions, center_grad, sub_increment)


def solution(mesh):
    return jax.shard_map(
        local,
        mesh=mesh,
        in_specs=(
            P(("blk", "grid"), None),
            P(("blk", "grid"), None),
            P(),
            P(),
            P(("blk", "grid")),
            P(("blk", "grid"), None),
            P(),
        ),
        out_specs=(P(), P(("blk", "grid"), None), P(("blk", "grid"), None)),
        check_vma=False,
    )
```

profile of v0, /device:TPU:0, one launch (start us, length us, event | category | flops | bytes accessed | tf_op | source)
XLA Modules:
  0.0 215.3 jit_solution(7999707913510482286)
XLA Ops:
  7.2 0.0 all-reduce.3.cloned.1.call-start
  7.2 1.0 multiply_reduce_fusion.2
  8.3 0.7 compare_and_fusion.1
  9.0 2.0 gather_fusion
  11.0 0.2 convert_select_fusion
  11.2 0.0 copy-start.2
  11.2 53.3 %all-reduce.4 = bf16[512,512]{1,0:T(8,128)(2,1)S(1)} all-reduce(f32[512,512]{1,0:T(8,128)S(1)} %convert_select_fusion), channel_id=1, replica_groups=mesh['blk'=2,'grid'=16] {'blk','grid'}, use_global_device_ids=true, to_apply=%region_0.1 | all-reduce | flops 262144 | bytes 1572864 | tf_op jit(solution)/shard_map/psum | solution.py:34
  64.5 0.2 multiply_reduce_fusion
  64.6 0.3 fusion.17
  65.0 1.8 fusion.35
  66.8 0.0 all-reduce.3.cloned.1.call-update
  66.8 0.6 gather_fusion.1
  67.4 39.6 %all_gather.7 = bf16[256,160]{1,0:T(8,128)(2,1)S(1)} all-gather(bf16[8,160]{1,0:T(8,128)(2,1)S(1)} %copy-done.3), channel_id=1, replica_groups=mesh['blk'=2,'grid'=16] {'blk','grid'}, dimensions={0}, use_global_device_ids=true | all-gather | bytes 84480 | tf_op jit(solution)/shard_map/all_gather | solution.py:42
  107.0 0.1 broadcast_select_fusion
  107.1 37.3 %all_gather.6 = bf16[256,512]{1,0:T(8,128)(2,1)S(1)} all-gather(bf16[8,512]{1,0:T(8,128)(2,1)S(1)} %broadcast_select_fusion), channel_id=1, replica_groups=mesh['blk'=2,'grid'=16] {'blk','grid'}, dimensions={0}, use_global_device_ids=true | all-gather | bytes 270336 | tf_op jit(solution)/shard_map/all_gather | solution.py:41
  144.4 0.1 multiply_reduce_fusion.1
  144.5 0.4 fusion.27
  144.9 0.7 fusion.9
  145.6 54.2 %all-reduce.3.cloned.1.call-done = f32[512,1000]{0,1:T(8,128)} async-done(((f32[512,1000]{0,1:T(8,128)}), f32[512,1000]{0,1:T(8,128)}) %all-reduce.3.cloned.1.call-update) | async-done | bytes 2048016 | tf_op jit(solution)/shard_map/psum | solution.py:37
  199.8 3.6 %convolution_multiply_fusion = f32[160,1000]{1,0:T(8,128)S(1)} fusion(f32[512,160]{1,0:T(8,128)S(1)} %fusion.9, f32[160]{0:T(256)S(1)} %copy-done.5, f32[512,1000]{0,1:T(8,128)} %all-reduce.3.cloned.1.call-done, s32[512]{0:T(512)S(1)} %copy-done.4), kind=kOutput, calls=%fused_computation.4 | convolution fusion | flops 985248000 | bytes 3018368 | tf_op jit(solution)/shard_map/dot_general | solution.py:49
  203.4 0.9 convolution_bitcast_fusion
  204.4 1.8 fusion.57
  206.2 1.1 convert_element_type.50
  207.3 1.1 fusion.8
  (17 shorter events, 0.1 us)
Async XLA Ops:
  7.2 1.8 copy-start
  7.2 192.6 %all-reduce.3.cloned.1.call-start = ((), (), s32[]{:S(2)}) async-start(), calls=%async_computation | async-start | bytes 4096000 | tf_op jit(solution)/shard_map/psum | solution.py:37
  11.2 53.8 %copy-start.2 = (f32[128,1000]{0,1:T(8,128)S(1)}, f32[128,1000]{0,1:T(8,128)}, u32[]{:S(2)}) copy-start(f32[128,1000]{0,1:T(8,128)} %param.8) | copy-start | bytes 1536004
  65.0 1.8 copy-start.6
  65.0 2.4 %copy-start.3 = (bf16[8,160]{1,0:T(8,128)(2,1)S(1)}, bf16[8,160]{1,0:T(8,128)(2,1)}, u32[]{:S(2)}) copy-start(bf16[8,160]{1,0:T(8,128)(2,1)} %param.12) | copy-start | bytes 7684
  66.8 133.0 %copy-start.4 = (s32[512]{0:T(512)S(1)}, s32[512]{0:T(512)}, u32[]{:S(2)}) copy-start(s32[512]{0:T(512)} %param.10) | copy-start | bytes 6148
  66.8 133.0 %copy-start.5 = (f32[160]{0:T(256)S(1)}, f32[160]{0:T(256)}, u32[]{:S(2)}) copy-start(f32[160]{0:T(256)} %param.13) | copy-start | bytes 1924
  199.8 6.4 %copy-start.1 = (f32[512,1000]{0,1:T(8,128)S(1)}, f32[512,1000]{0,1:T(8,128)}, u32[]{:S(2)}) copy-start(f32[512,1000]{0,1:T(8,128)} %all-reduce.3.cloned.1.call-done) | copy-start | bytes 6144004
Sparse Core Ops, SparseCore 0:
  66.9 132.8 all-reduce.2
where the time goes:
time: 215 us
  blocking collectives  130 us (60%)
  waiting for transfers between devices  54.2 us (25%)
  between operations  14.2 us (7%)
  matrix products  10.6 us (5%)
  other arithmetic  3.42 us (2%)
  local copies, waits for them, and re-layouts  2.58 us (1%)
    psum x1, waiting for transfers between devices, local(): total = lax.psum(partial_out, ('blk', 'grid'))  54.2 us
    psum x1, blocking collectives, local(): batch = lax.psum(picked, ('blk', 'grid')).astype(jnp.bfloat16)  53.3 us
    all_gather x1, blocking collectives, local(): vec_rows = lax.all_gather(eigvecs, ('blk', 'grid'), axis=0, tiled=True)  39.6 us
    all_gather x1, blocking collectives, local(): sub_rows = lax.all_gather(subset_here, ('blk', 'grid'), axis=0, tiled=True)  37.3 us
  transfers between devices with their start and end apart: 1, of which 1 were waited for; matrix products, arithmetic and copies ran while one was open for 1% of the time, Pallas kernels for 0%

commit v1 on v0

--- a/solution.py
+++ b/solution.py
@@ -31,7 +31,7 @@
     within = batch_index % held
     picked = jnp.take(centers, within, axis=0).astype(jnp.float32)
     picked = jnp.where((owner == myself)[:, None], picked, 0.0)
-    batch = lax.psum(picked, ("blk", "grid")).astype(jnp.bfloat16)
+    batch = jnp.sum(lax.all_gather(picked, ("blk", "grid")), axis=0).astype(jnp.bfloat16)
     kbz = kernel(batch, centers).astype(jnp.bfloat16)
     partial_out = jnp.dot(kbz, weights.astype(jnp.bfloat16), preferred_element_type=jnp.float32)
     total = lax.psum(partial_out, ("blk", "grid"))

time: 215 us -> 372 us (1.73)
  waiting for transfers between devices: 54.2 us -> 251 us
  blocking collectives: 130 us -> 76.6 us
  other arithmetic: 3.42 us -> 15.8 us
    all_gather x0 -> x1, waiting for transfers between devices: none -> 197 us  [local(): lax.all_gather(picked, ('blk', 'grid'))]
    psum x1 -> x0, blocking collectives: 53.3 us -> none  [local(): batch = lax.psum(picked, ('blk', 'grid')).astype(jnp.bfloat16)]
    reduce_sum x0 -> x1, other arithmetic: none -> 12.3 us  [local(): jnp.sum(lax.all_gather(picked, ('blk', 'grid')), axis=0)]
  transfers between devices with their start and end apart: 1 -> 2, of which waited for: 1 -> 2; matrix products, arithmetic and copies ran while one was open for 1% -> 1% of each run, Pallas kernels for 0% -> 0%
where the time goes in v1:
time: 372 us
  waiting for transfers between devices  251 us (67%)
  blocking collectives  76.6 us (21%)
  other arithmetic  15.8 us (4%)
  between operations  14.2 us (4%)
  matrix products  9.99 us (3%)
  local copies, waits for them, and re-layouts  4.03 us (1%)
    all_gather x1, waiting for transfers between devices, local(): lax.all_gather(picked, ('blk', 'grid'))  197 us
    psum x1, waiting for transfers between devices, local(): total = lax.psum(partial_out, ('blk', 'grid'))  54 us
    all_gather x1, blocking collectives, local(): vec_rows = lax.all_gather(eigvecs, ('blk', 'grid'), axis=0, tiled=True)  39.3 us
    all_gather x1, blocking collectives, local(): sub_rows = lax.all_gather(subset_here, ('blk', 'grid'), axis=0, tiled=True)  37.3 us
    reduce_sum x1, other arithmetic, local(): jnp.sum(lax.all_gather(picked, ('blk', 'grid')), axis=0)  12.3 us
  transfers between devices with their start and end apart: 2, of which 2 were waited for; matrix products, arithmetic and copies ran while one was open for 1% of the time, Pallas kernels for 0%

profile of v1, /device:TPU:0, one launch (start us, length us, event | category | flops | bytes accessed | tf_op | source)
XLA Modules:
  0.0 371.7 jit_solution(13962201274848142599)
XLA Ops:
  7.2 0.7 compare_and_fusion.1
  7.9 2.9 gather_fusion
  10.9 1.2 convert_select_fusion
  12.1 0.0 all-reduce.2.cloned.1.call-start
  12.1 0.1 multiply_reduce_fusion.2
  12.3 196.8 %all-gather.2.cloned.1.call-done = f32[32,512,512]{2,1,0:T(8,128)} async-done(((f32[1,512,512]{2,1,0:T(8,128)}), f32[32,512,512]{2,1,0:T(8,128)}) %all-gather.2.cloned.1.call-update) | async-done | bytes 33554448 | tf_op jit(solution)/shard_map/all_gather | solution.py:34
  209.1 12.3 %reduce_sum.35 = bf16[512,512]{1,0:T(8,128)(2,1)S(1)} reduce(f32[32,512,512]{2,1,0:T(8,128)} %all-gather.2.cloned.1.call-done, f32[]{:T(128)} %constant.80.clone.1), dimensions={0}, to_apply=%region_0.1 | reduce | flops 8126464 | bytes 34078724 | tf_op jit(solution)/shard_map/reduce_sum | solution.py:34
  221.5 0.2 multiply_reduce_fusion
  221.6 0.3 fusion.17
  222.0 0.5 copy-done.2
  222.5 1.8 fusion.35
  224.3 0.6 gather_fusion.1
  224.9 39.3 %all_gather.12 = bf16[256,160]{1,0:T(8,128)(2,1)S(1)} all-gather(bf16[8,160]{1,0:T(8,128)(2,1)S(1)} %copy-done.3), channel_id=1, replica_groups=mesh['blk'=2,'grid'=16] {'blk','grid'}, dimensions={0}, use_global_device_ids=true | all-gather | bytes 84480 | tf_op jit(solution)/shard_map/all_gather | solution.py:42
  264.2 0.1 broadcast_select_fusion
  264.3 37.3 %all_gather.11 = bf16[256,512]{1,0:T(8,128)(2,1)S(1)} all-gather(bf16[8,512]{1,0:T(8,128)(2,1)S(1)} %broadcast_select_fusion), channel_id=1, replica_groups=mesh['blk'=2,'grid'=16] {'blk','grid'}, dimensions={0}, use_global_device_ids=true | all-gather | bytes 270336 | tf_op jit(solution)/shard_map/all_gather | solution.py:41
  301.6 0.1 multiply_reduce_fusion.1
  301.7 0.4 fusion.27
  302.2 0.7 fusion.9
  302.9 54.0 %all-reduce.2.cloned.1.call-done = f32[512,1000]{0,1:T(8,128)} async-done(((f32[512,1000]{0,1:T(8,128)}), f32[512,1000]{0,1:T(8,128)}) %all-reduce.2.cloned.1.call-update) | async-done | bytes 2048016 | tf_op jit(solution)/shard_map/psum | solution.py:37
  357.0 2.8 convolution_multiply_fusion
  359.8 0.9 convolution_bitcast_fusion
  360.7 1.8 fusion.57
  362.6 1.1 convert_element_type.57
  363.7 1.1 fusion.8
  (20 shorter events, 0.1 us)
Async XLA Ops:
  7.2 202.0 %all-gather.2.cloned.1.call-start = ((), (), s32[]{:S(2)}) async-start(), calls=%async_computation | async-start | bytes 34603008 | tf_op jit(solution)/shard_map/all_gather | solution.py:34
  10.8 1.3 copy-start
  10.9 1.4 copy-start.6
  12.1 344.9 %all-reduce.2.cloned.1.call-start = ((), (), s32[]{:S(2)}) async-start(), calls=%async_computation.1 | async-start | bytes 4096000 | tf_op jit(solution)/shard_map/psum | solution.py:37
  221.5 1.0 copy-start.2
  222.5 2.4 copy-start.3
  224.3 132.7 %copy-start.4 = (s32[512]{0:T(512)S(1)}, s32[512]{0:T(512)}, u32[]{:S(2)}) copy-start(s32[512]{0:T(512)} %param.10) | copy-start | bytes 6148
  224.3 132.7 %copy-start.5 = (f32[160]{0:T(256)S(1)}, f32[160]{0:T(256)}, u32[]{:S(2)}) copy-start(f32[160]{0:T(256)} %param.13) | copy-start | bytes 1924
  357.0 5.6 %copy-start.1 = (f32[512,1000]{0,1:T(8,128)S(1)}, f32[512,1000]{0,1:T(8,128)}, u32[]{:S(2)}) copy-start(f32[512,1000]{0,1:T(8,128)} %all-reduce.2.cloned.1.call-done) | copy-start | bytes 6144004
Sparse Core Ops, SparseCore 0:
  12.2 196.8 all-gather.1
  224.4 132.5 all-reduce.1

commit v2 on v0

--- a/solution.py
+++ b/solution.py
@@ -31,7 +31,7 @@
     within = batch_index % held
     picked = jnp.take(centers, within, axis=0).astype(jnp.float32)
     picked = jnp.where((owner == myself)[:, None], picked, 0.0)
-    batch = lax.psum(picked, ("blk", "grid")).astype(jnp.bfloat16)
+    batch = lax.psum(lax.psum(picked, "grid"), "blk").astype(jnp.bfloat16)
     kbz = kernel(batch, centers).astype(jnp.bfloat16)
     partial_out = jnp.dot(kbz, weights.astype(jnp.bfloat16), preferred_element_type=jnp.float32)
     total = lax.psum(partial_out, ("blk", "grid"))

time: 215 us -> 288 us (1.34)
  waiting for transfers between devices: 54.2 us -> 151 us
  blocking collectives: 130 us -> 105 us
    psum x0 -> x1, waiting for transfers between devices: none -> 96.4 us  [local(): batch = lax.psum(lax.psum(picked, 'grid'), 'blk').astype(jnp.bfloat16)]
    psum x1, blocking collectives: 53.3 us -> 28 us  [local(): batch = lax.psum(lax.psum(picked, 'grid'), 'blk').astype(jnp.bfloat16)]
  transfers between devices with their start and end apart: 1 -> 2, of which waited for: 1 -> 2; matrix products, arithmetic and copies ran while one was open for 1% -> 1% of each run, Pallas kernels for 0% -> 0%
where the time goes in v2:
time: 288 us; the launch traced here: 287 us
  waiting for transfers between devices  151 us (52%)
  blocking collectives  105 us (36%)
  between operations  14.2 us (5%)
  matrix products  10.6 us (4%)
  other arithmetic  3.54 us (1%)
  local copies, waits for them, and re-layouts  3.52 us (1%)
    psum x1, waiting for transfers between devices, local(): batch = lax.psum(lax.psum(picked, 'grid'), 'blk').astype(jnp.bfloat16)  96.4 us
    psum x1, waiting for transfers between devices, local(): total = lax.psum(partial_out, ('blk', 'grid'))  54.1 us
    all_gather x1, blocking collectives, local(): vec_rows = lax.all_gather(eigvecs, ('blk', 'grid'), axis=0, tiled=True)  39.6 us
    all_gather x1, blocking collectives, local(): sub_rows = lax.all_gather(subset_here, ('blk', 'grid'), axis=0, tiled=True)  37.3 us
    psum x1, blocking collectives, local(): batch = lax.psum(lax.psum(picked, 'grid'), 'blk').astype(jnp.bfloat16)  28 us
  transfers between devices with their start and end apart: 2, of which 2 were waited for; matrix products, arithmetic and copies ran while one was open for 1% of the time, Pallas kernels for 0%

profile of v2, /device:TPU:0, one launch (start us, length us, event | category | flops | bytes accessed | tf_op | source)
XLA Modules:
  0.0 287.5 jit_solution(11561156697388743720)
XLA Ops:
  7.2 0.0 all-reduce.4.cloned.1.call-start
  7.2 0.7 compare_and_fusion.1
  7.9 2.9 %gather_fusion = bf16[512,512]{1,0:T(8,128)(2,1)S(1)} fusion(bf16[128,512]{1,0:T(8,128)(2,1)} %param.7, s32[1024]{0:T(1024)S(1)} %pad_clamp_fusion.1), kind=kCustom, calls=%fused_computation | custom fusion | bytes 1050624 | tf_op jit(solution)/shard_map/jit(_take)/gather | solution.py:32
  10.9 1.2 convert_select_fusion
  12.1 0.0 all-reduce.6.cloned.1.call-start
  12.2 0.1 multiply_reduce_fusion.2
  12.3 96.4 %all-reduce.4.cloned.1.call-done = f32[512,512]{1,0:T(8,128)} async-done(((f32[512,512]{1,0:T(8,128)}), f32[512,512]{1,0:T(8,128)}) %all-reduce.4.cloned.1.call-update) | async-done | bytes 1048592 | tf_op jit(solution)/shard_map/psum | solution.py:34
  108.7 28.0 %all-reduce.7 = bf16[512,512]{1,0:T(8,128)(2,1)S(1)} all-reduce(f32[512,512]{1,0:T(8,128)} %all-reduce.4.cloned.1.call-done), channel_id=1, replica_groups=mesh['blk'=2,'grid'=16] {'blk'}, use_global_device_ids=true, to_apply=%region_1.2 | all-reduce | flops 262144 | bytes 1572864 | tf_op jit(solution)/shard_map/psum | solution.py:34
  136.8 0.2 multiply_reduce_fusion
  137.0 0.3 fusion.17
  137.3 1.7 fusion.35
  139.1 0.6 gather_fusion.1
  139.7 39.6 %all_gather.7 = bf16[256,160]{1,0:T(8,128)(2,1)S(1)} all-gather(bf16[8,160]{1,0:T(8,128)(2,1)S(1)} %copy-done.3), channel_id=1, replica_groups=mesh['blk'=2,'grid'=16] {'blk','grid'}, dimensions={0}, use_global_device_ids=true | all-gather | bytes 84480 | tf_op jit(solution)/shard_map/all_gather | solution.py:42
  179.3 0.1 broadcast_select_fusion
  179.4 37.3 %all_gather.6 = bf16[256,512]{1,0:T(8,128)(2,1)S(1)} all-gather(bf16[8,512]{1,0:T(8,128)(2,1)S(1)} %broadcast_select_fusion), channel_id=1, replica_groups=mesh['blk'=2,'grid'=16] {'blk','grid'}, dimensions={0}, use_global_device_ids=true | all-gather | bytes 270336 | tf_op jit(solution)/shard_map/all_gather | solution.py:41
  216.7 0.1 multiply_reduce_fusion.1
  216.9 0.4 fusion.27
  217.2 0.7 fusion.9
  217.9 54.1 %all-reduce.6.cloned.1.call-done = f32[512,1000]{0,1:T(8,128)} async-done(((f32[512,1000]{0,1:T(8,128)}), f32[512,1000]{0,1:T(8,128)}) %all-reduce.6.cloned.1.call-update) | async-done | bytes 2048016 | tf_op jit(solution)/shard_map/psum | solution.py:37
  272.0 3.6 %convolution_multiply_fusion = f32[160,1000]{1,0:T(8,128)S(1)} fusion(f32[512,160]{1,0:T(8,128)S(1)} %fusion.9, f32[160]{0:T(256)S(1)} %copy-done.5, f32[512,1000]{0,1:T(8,128)} %all-reduce.6.cloned.1.call-done, s32[512]{0:T(512)S(1)} %copy-done.4), kind=kOutput, calls=%fused_computation.4 | convolution fusion | flops 985248000 | bytes 3018368 | tf_op jit(solution)/shard_map/dot_general | solution.py:49
  275.6 0.9 convolution_bitcast_fusion
  276.6 1.8 fusion.57
  278.4 1.1 convert_element_type.50
  279.5 1.1 fusion.8
  (20 shorter events, 0.1 us)
Async XLA Ops:
  7.2 101.6 %all-reduce.4.cloned.1.call-start = ((), (), s32[]{:S(2)}) async-start(), calls=%async_computation | async-start | bytes 2097152 | tf_op jit(solution)/shard_map/psum | solution.py:34
  10.8 1.3 copy-start
  10.9 1.5 copy-start.6
  12.1 125.2 %copy-start.2 = (f32[128,1000]{0,1:T(8,128)S(1)}, f32[128,1000]{0,1:T(8,128)}, u32[]{:S(2)}) copy-start(f32[128,1000]{0,1:T(8,128)} %param.8) | copy-start | bytes 1536004
  12.1 259.9 %all-reduce.6.cloned.1.call-start = ((), (), s32[]{:S(2)}) async-start(), calls=%async_computation.1 | async-start | bytes 4096000 | tf_op jit(solution)/shard_map/psum | solution.py:37
  137.3 2.4 copy-start.3
  139.1 132.9 %copy-start.4 = (s32[512]{0:T(512)S(1)}, s32[512]{0:T(512)}, u32[]{:S(2)}) copy-start(s32[512]{0:T(512)} %param.10) | copy-start | bytes 6148
  139.1 132.9 %copy-start.5 = (f32[160]{0:T(256)S(1)}, f32[160]{0:T(256)}, u32[]{:S(2)}) copy-start(f32[160]{0:T(256)} %param.13) | copy-start | bytes 1924
  272.0 6.4 %copy-start.1 = (f32[512,1000]{0,1:T(8,128)S(1)}, f32[512,1000]{0,1:T(8,128)}, u32[]{:S(2)}) copy-start(f32[512,1000]{0,1:T(8,128)} %all-reduce.6.cloned.1.call-done) | copy-start | bytes 6144004
Sparse Core Ops, SparseCore 0:
  12.3 96.4 all-reduce.3
  139.2 132.7 all-reduce.5

commit v3 on v0

--- a/solution.py
+++ b/solution.py
@@ -34,7 +34,7 @@
     batch = lax.psum(picked, ("blk", "grid")).astype(jnp.bfloat16)
     kbz = kernel(batch, centers).astype(jnp.bfloat16)
     partial_out = jnp.dot(kbz, weights.astype(jnp.bfloat16), preferred_element_type=jnp.float32)
-    total = lax.psum(partial_out, ("blk", "grid"))
+    total = lax.psum(lax.psum(partial_out, "blk"), "grid")
     predictions = total.astype(jnp.bfloat16)
     resid = (total - one_hot(labels, classes)).astype(jnp.bfloat16)
     subset_here = jnp.take(centers, sub_index, axis=0)

time: 215 us -> 245 us (1.14)
  waiting for transfers between devices: 54.2 us -> 81.6 us
    psum x1 -> x2, waiting for transfers between devices: 54.2 us -> 81.6 us  [local(): total = lax.psum(lax.psum(partial_out, 'blk'), 'grid')]
  transfers between devices with their start and end apart: 1 -> 2, of which waited for: 1 -> 2; matrix products, arithmetic and copies ran while one was open for 1% -> 1% of each run, Pallas kernels for 0% -> 0%
where the time goes in v3:
time: 245 us
  blocking collectives  132 us (54%)
  waiting for transfers between devices  81.6 us (33%)
  between operations  14.2 us (6%)
  matrix products  10.6 us (4%)
  other arithmetic  3.42 us (1%)
  local copies, waits for them, and re-layouts  2.58 us (1%)
    psum x2, waiting for transfers between devices, local(): total = lax.psum(lax.psum(partial_out, 'blk'), 'grid')  81.6 us
    psum x1, blocking collectives, local(): batch = lax.psum(picked, ('blk', 'grid')).astype(jnp.bfloat16)  53.3 us
    all_gather x1, blocking collectives, local(): vec_rows = lax.all_gather(eigvecs, ('blk', 'grid'), axis=0, tiled=True)  41.4 us
    all_gather x1, blocking collectives, local(): sub_rows = lax.all_gather(subset_here, ('blk', 'grid'), axis=0, tiled=True)  37.4 us
  transfers between devices with their start and end apart: 2, of which 2 were waited for; matrix products, arithmetic and copies ran while one was open for 1% of the time, Pallas kernels for 0%

profile of v3, /device:TPU:0, one launch (start us, length us, event | category | flops | bytes accessed | tf_op | source)
XLA Modules:
  0.0 244.6 jit_solution(3535265286102860149)
XLA Ops:
  7.2 0.0 all-reduce.4.cloned.1.call-start
  7.2 1.0 multiply_reduce_fusion.2
  8.3 0.7 compare_and_fusion.1
  9.0 2.0 gather_fusion
  11.0 0.2 convert_select_fusion
  11.2 53.3 %all-reduce.7 = bf16[512,512]{1,0:T(8,128)(2,1)S(1)} all-reduce(f32[512,512]{1,0:T(8,128)S(1)} %convert_select_fusion), channel_id=1, replica_groups=mesh['blk'=2,'grid'=16] {'blk','grid'}, use_global_device_ids=true, to_apply=%region_0.1 | all-reduce | flops 262144 | bytes 1572864 | tf_op jit(solution)/shard_map/psum | solution.py:34
  64.5 0.2 multiply_reduce_fusion
  64.6 0.3 fusion.17
  65.0 1.8 fusion.35
  66.8 0.0 all-reduce.6.cloned.1.call-start
  66.9 60.4 %all-reduce.4.cloned.1.call-done = f32[512,1000]{0,1:T(8,128)} async-done(((f32[512,1000]{0,1:T(8,128)}), f32[512,1000]{0,1:T(8,128)}) %all-reduce.4.cloned.1.call-update) | async-done | bytes 2048016 | tf_op jit(solution)/shard_map/psum | solution.py:37
  127.4 0.6 gather_fusion.1
  127.9 41.4 %all_gather.7 = bf16[256,160]{1,0:T(8,128)(2,1)S(1)} all-gather(bf16[8,160]{1,0:T(8,128)(2,1)S(1)} %copy-done.3), channel_id=1, replica_groups=mesh['blk'=2,'grid'=16] {'blk','grid'}, dimensions={0}, use_global_device_ids=true | all-gather | bytes 84480 | tf_op jit(solution)/shard_map/all_gather | solution.py:42
  169.3 0.1 broadcast_select_fusion
  169.4 37.4 %all_gather.6 = bf16[256,512]{1,0:T(8,128)(2,1)S(1)} all-gather(bf16[8,512]{1,0:T(8,128)(2,1)S(1)} %broadcast_select_fusion), channel_id=1, replica_groups=mesh['blk'=2,'grid'=16] {'blk','grid'}, dimensions={0}, use_global_device_ids=true | all-gather | bytes 270336 | tf_op jit(solution)/shard_map/all_gather | solution.py:41
  206.8 0.1 multiply_reduce_fusion.1
  206.9 0.4 fusion.27
  207.3 0.7 fusion.9
  208.0 21.2 %all-reduce.6.cloned.1.call-done = f32[512,1000]{0,1:T(8,128)} async-done(((f32[512,1000]{0,1:T(8,128)}), f32[512,1000]{0,1:T(8,128)}) %all-reduce.6.cloned.1.call-update) | async-done | bytes 2048016 | tf_op jit(solution)/shard_map/psum | solution.py:37
  229.2 3.6 %convolution_multiply_fusion = f32[160,1000]{1,0:T(8,128)S(1)} fusion(f32[512,160]{1,0:T(8,128)S(1)} %fusion.9, f32[160]{0:T(256)S(1)} %copy-done.5, f32[512,1000]{0,1:T(8,128)} %all-reduce.6.cloned.1.call-done, s32[512]{0:T(512)S(1)} %copy-done.4), kind=kOutput, calls=%fused_computation.4 | convolution fusion | flops 985248000 | bytes 3018368 | tf_op jit(solution)/shard_map/dot_general | solution.py:49
  232.8 0.9 convolution_bitcast_fusion
  233.7 1.8 fusion.57
  235.6 1.1 convert_element_type.50
  236.7 1.1 fusion.8
  (20 shorter events, 0.1 us)
Async XLA Ops:
  7.2 1.8 copy-start
  7.2 120.1 %all-reduce.4.cloned.1.call-start = ((), (), s32[]{:S(2)}) async-start(), calls=%async_computation | async-start | bytes 4096000 | tf_op jit(solution)/shard_map/psum | solution.py:37
  11.2 53.8 %copy-start.2 = (f32[128,1000]{0,1:T(8,128)S(1)}, f32[128,1000]{0,1:T(8,128)}, u32[]{:S(2)}) copy-start(f32[128,1000]{0,1:T(8,128)} %param.8) | copy-start | bytes 1536004
  65.0 1.8 copy-start.6
  66.7 61.2 %copy-start.3 = (bf16[8,160]{1,0:T(8,128)(2,1)S(1)}, bf16[8,160]{1,0:T(8,128)(2,1)}, u32[]{:S(2)}) copy-start(bf16[8,160]{1,0:T(8,128)(2,1)} %param.12) | copy-start | bytes 7684
  66.8 162.4 %all-reduce.6.cloned.1.call-start = ((), (), s32[]{:S(2)}) async-start(), calls=%async_computation.1 | async-start | bytes 4096000 | tf_op jit(solution)/shard_map/psum | solution.py:37
  127.3 101.9 %copy-start.4 = (s32[512]{0:T(512)S(1)}, s32[512]{0:T(512)}, u32[]{:S(2)}) copy-start(s32[512]{0:T(512)} %param.10) | copy-start | bytes 6148
  127.3 101.9 %copy-start.5 = (f32[160]{0:T(256)S(1)}, f32[160]{0:T(256)}, u32[]{:S(2)}) copy-start(f32[160]{0:T(256)} %param.13) | copy-start | bytes 1924
  229.2 6.4 %copy-start.1 = (f32[512,1000]{0,1:T(8,128)S(1)}, f32[512,1000]{0,1:T(8,128)}, u32[]{:S(2)}) copy-start(f32[512,1000]{0,1:T(8,128)} %all-reduce.6.cloned.1.call-done) | copy-start | bytes 6144004
Sparse Core Ops, SparseCore 0:
  66.9 60.3 all-reduce.3
  130.8 98.2 all-reduce.5
